TPU v7x, 512 devices: a whole 4x4x16 slice. The times are simulated.
512 devices in a mesh: space: 64 (over z, x_lo, core), tm: 8 (over x_hi, y).
Axes of the slice: x: 4 (x_hi: 2, x_lo: 2; x = x_hi * 2 + x_lo), y: 4, z: 16, core: 2. Of those that a mesh axis runs over, the one named last changes fastest.
Arguments:
- snapshots: bfloat16 [131072, 8192], P('space', 'tm'), may hold values from -30 to 30
- omega: int32 [32, 8192], P(None, 'tm'), may hold values from -1 to 1, as said below
Outputs:
- sketch: bfloat16 [32, 131072], P(None, 'space')
- coefficients: float32 [32, 8192], P(None, 'tm')
Inputs may be any that keep to these rules, and one draw needn't show every extreme that they name: `omega`: every entry is -1 or 1.
All inputs are finite; a program needn't handle non-finite values.
Results may differ from a plain program's by a relative error of at most 0.0028.
Values may be sent and summed in bfloat16 or wider, within the bound.
A program may use at most 64 MiB of HBM per device.

v0:
```python
import jax
import jax.numpy as jnp
from jax import lax
from jax.sharding import PartitionSpec as P

SNAP = 8192


def per_device(snapshots, omega):
    signs = omega.astype(jnp.bfloat16)
    partial_sums = lax.dot_general(
        signs, snapshots, (((1,), (1,)), ((), ())), preferred_element_type=jnp.float32
    )
    factor = SNAP ** (-0.5)
    summed = lax.psum(partial_sums, "tm")
    sketch = (summed * factor).astype(jnp.bfloat16)
    gram_part = lax.dot_general(
        sketch, sketch, (((1,), (1,)), ((), ())), preferred_element_type=jnp.float32
    )
    proj_part = jnp.dot(sketch, snapshots, preferred_element_type=jnp.float32)
    gram = lax.psum(gram_part, "space")
    projection = lax.psum(proj_part, "space")
    lower = jnp.linalg.cholesky(gram)
    coefficients = jax.scipy.linalg.solve_triangular(lower, projection, lower=True)
    return (sketch, coefficients)


def solution(mesh):
    placed = (P("space", "tm"), P(None, "tm"))
    return jax.shard_map(
        per_device,
        mesh=mesh,
        in_specs=placed,
        out_specs=(P(None, "space"), P(None, "tm")),
        check_vma=False,
    )
```

profile of v0, /device:TPU:1, one launch (start us, length us, event | category | flops | bytes accessed | tf_op | source)
XLA Modules:
  0.0 724.2 jit_solution(13899461857553801861)
XLA Ops:
  7.2 0.0 all-reduce.3.cloned.1.call-start
  7.2 4.3 fusion
  11.5 0.0 all-reduce.3.cloned.1.call-update
  11.5 0.0 all-reduce.5.cloned.1.call-start
  11.6 100.2 %all-reduce.3.cloned.1.call-done = f32[32,2048]{1,0:T(8,128)} async-done(((f32[32,2048]{1,0:T(8,128)}), f32[32,2048]{1,0:T(8,128)}) %all-reduce.3.cloned.1.call-update) | async-done | bytes 262160 | tf_op jit(solution)/shard_map/psum | solution.py:15
  111.8 1.0 multiply_convert_fusion
  112.7 0.0 copy-start
  112.8 0.2 fusion.6
  112.9 3.7 fusion.7
  116.6 209.6 %psum.22 = f32[32,32]{0,1:T(8,128)S(1)} all-reduce(f32[32,32]{0,1:T(8,128)S(1)} %fusion.6), channel_id=1, replica_groups=mesh['space'=64,'tm'=8] {'space'}, use_global_device_ids=true, to_apply=%region_1.0 | all-reduce | flops 1024 | bytes 8192 | tf_op jit(solution)/shard_map/psum | solution.py:21
  326.2 0.1 copy.5
  326.3 2.9 cholesky.16
  329.3 0.6 compare_reduce_fusion
  329.9 0.0 all-reduce.5.cloned.1.call-update
  329.9 0.6 fusion.2
  330.5 2.4 custom-call.7
  332.9 382.6 %all-reduce.5.cloned.1.call-done = f32[32,1024]{1,0:T(8,128)} async-done(((f32[32,1024]{1,0:T(8,128)}), f32[32,1024]{1,0:T(8,128)}) %all-reduce.5.cloned.1.call-update) | async-done | bytes 131088 | tf_op jit(solution)/shard_map/psum | solution.py:22
  715.5 1.9 fusion.3
  717.4 0.0 copy-done
  (2 shorter events, 0.0 us)
Async XLA Ops:
  7.2 104.6 %all-reduce.3.cloned.1.call-start = ((), (), s32[]{:S(2)}) async-start(), calls=%async_computation | async-start | bytes 524288 | tf_op jit(solution)/shard_map/psum | solution.py:15
  11.5 704.0 %all-reduce.5.cloned.1.call-start = ((), (), s32[]{:S(2)}) async-start(), calls=%async_computation.1 | async-start | bytes 262144 | tf_op jit(solution)/shard_map/psum | solution.py:22
  112.7 604.7 %copy-start = (bf16[32,2048]{1,0:T(8,128)(2,1)}, bf16[32,2048]{1,0:T(8,128)(2,1)S(1)}, u32[]{:S(2)}) copy-start(bf16[32,2048]{1,0:T(8,128)(2,1)S(1)} %multiply_convert_fusion) | copy-start | bytes 393220
Sparse Core Ops, SparseCore 0:
  11.7 100.0 all-reduce.2
  330.0 385.4 all-reduce.4
where the time goes:
time: 724 us
  waiting for transfers between devices  483 us (67%)
  blocking collectives  210 us (29%)
  between operations  14.1 us (2%)
  matrix products  10 us (1%)
  other arithmetic  7.57 us (1%)
    psum x1, waiting for transfers between devices, per_device(): projection = lax.psum(proj_part, 'space')  383 us
    psum x1, blocking collectives, per_device(): gram = lax.psum(gram_part, 'space')  210 us
    psum x1, waiting for transfers between devices, per_device(): summed = lax.psum(partial_sums, 'tm')  100 us
  transfers between devices with their start and end apart: 2, of which 2 were waited for; matrix products, arithmetic and copies ran while one was open for 0% of the time, Pallas kernels for 0%

commit v1 on v0

v1 whole, which is shorter than its diff:
```python
import jax
import jax.numpy as jnp
from jax import lax
from jax.experimental import pallas as pl
from jax.experimental.pallas import tpu as pltpu
from jax.sharding import PartitionSpec as P

MESH = pl.DeviceIdType.MESH
SNAP = 8192
K = 32
TM_FAR = ((1, 2), (1, 1), (1, 3), (1, 0), (0, 2), (0, 1), (0, 3))
OCT_FAR = ((1, 1, 0), (1, 1, 1), (1, 0, 0), (1, 0, 1), (0, 1, 0), (0, 1, 1), (0, 0, 1))
Z_FAR = (4, 3, 5, 2, 6, 1, 7)


def flip(bit, f):
    return (bit + f) % 2


def kernel(
    snap, omega, sketch_out, coef_out,
    a, om, part, rs, sk, pp, r8, zb, cb, g8, gz,
    in_sem, om_sem, out_sem,
    rs_send, rs_recv, ag_send, ag_recv, p8_send, p8_recv, z_send, z_recv,
    c8_send, c8_recv, g8_send, g8_recv, gz_send, gz_recv,
):
    s, t = lax.axis_index("space"), lax.axis_index("tm")
    z, xl, c = s // 4, (s // 2) % 2, s % 2
    xh, y = t // 4, t % 4
    zh, zp = z // 2, z % 2
    m = zp * 4 + xl * 2 + c
    rows = a.shape[1]

    def tm_of(off):
        return flip(xh, off[0]) * 4 + (y + off[1]) % 4

    def oct_of(f):
        q = flip(zp, f[0]) * 4 + flip(xl, f[1]) * 2 + flip(c, f[2])
        return q, (zh * 8 + q, t)

    def z_of(j):
        w = (zh + j) % 8
        return w, (w * 8 + m, t)

    om_copy = pltpu.make_async_copy(omega, om, om_sem)
    om_copy.start()
    order = [tm_of(off) for off in TM_FAR] + [t]
    loads = []
    for i, d in enumerate(order):
        cp = pltpu.make_async_copy(
            snap.at[pl.ds(pl.multiple_of(d * rows, rows), rows), :], a.at[d], in_sem.at[i]
        )
        cp.start()
        loads.append(cp)

    barrier = pltpu.get_barrier_semaphore()
    peers = [(s, tm_of(off)) for off in TM_FAR]
    peers += [oct_of(f)[1] for f in OCT_FAR] + [z_of(j)[1] for j in Z_FAR]
    for peer in peers:
        pl.semaphore_signal(barrier, inc=1, device_id=peer, device_id_type=MESH)

    def send(src, dst, send_sem, recv_sem, peer):
        return pltpu.make_async_remote_copy(
            src_ref=src, dst_ref=dst, send_sem=send_sem, recv_sem=recv_sem,
            device_id=peer, device_id_type=MESH,
        )

    om_copy.wait()
    signs = om[...].astype(jnp.float32).astype(jnp.bfloat16)
    for i, d in enumerate(order):
        loads[i].wait()
        part[i] = lax.dot_general(
            signs, a[d], (((1,), (1,)), ((), ())), preferred_element_type=jnp.float32
        )
    pl.semaphore_wait(barrier, len(peers))
    sent = []
    rs_copies = []
    for i, off in enumerate(TM_FAR):
        cp = send(part.at[i], rs.at[i], rs_send.at[i], rs_recv.at[i], (s, order[i]))
        cp.start()
        rs_copies.append(cp)
    sent += rs_copies

    total = part[7]
    for i in (5, 6, 4, 3, 1, 2, 0):
        rs_copies[i].wait_recv()
        total = total + rs[i]
    factor = SNAP ** (-0.5)
    sk[t] = (total * factor).astype(jnp.bfloat16)
    for i, off in enumerate(TM_FAR):
        cp = send(sk.at[t], sk.at[t], ag_send.at[i], ag_recv.at[t], (s, order[i]))
        cp.start()
        sent.append(cp)

    proj = None
    gram = None
    outs = []
    for i in (7, 5, 6, 4, 3, 1, 2, 0):
        d = order[i]
        if i < 7:
            send(sk.at[d], sk.at[d], ag_send.at[i], ag_recv.at[d], (s, d)).wait_recv()
        cp = pltpu.make_async_copy(
            sk.at[d], sketch_out.at[:, pl.ds(pl.multiple_of(d * rows, rows), rows)], out_sem.at[i]
        )
        cp.start()
        outs.append(cp)
        block = sk[d]
        wide = jnp.concatenate([block] * 4, axis=0)
        g = lax.dot_general(
            block, wide, (((1,), (1,)), ((), ())), preferred_element_type=jnp.float32
        )
        p = jnp.dot(block, a[d], preferred_element_type=jnp.float32)
        gram = g if gram is None else gram + g
        proj = p if proj is None else proj + p

    lane8 = lax.broadcasted_iota(jnp.int32, (8, 128), 1) // K
    packed = jnp.zeros((8, 128), jnp.float32)
    for b in range(4):
        packed = jnp.where(lane8 == b, gram[8 * b : 8 * b + 8], packed)
    g8[m] = packed
    for i, f in enumerate(OCT_FAR):
        q, peer = oct_of(f)
        cp = send(g8.at[m], g8.at[m], g8_send.at[i], g8_recv.at[m], peer)
        cp.start()
        sent.append(cp)
    for q in range(8):
        pp[q] = proj[:, 128 * q : 128 * q + 128]
    r8[m] = pp[m]
    for i, f in enumerate(OCT_FAR):
        q, peer = oct_of(f)
        cp = send(pp.at[q], r8.at[m], p8_send.at[i], p8_recv.at[m], peer)
        cp.start()
        sent.append(cp)

    for i, f in enumerate(OCT_FAR):
        q, peer = oct_of(f)
        send(g8.at[q], g8.at[q], g8_send.at[i], g8_recv.at[q], peer).wait_recv()
    gsum = g8[0]
    for q in range(1, 8):
        gsum = gsum + g8[q]
    gz[zh] = gsum
    for i, j in enumerate(Z_FAR):
        w, peer = z_of(j)
        cp = send(gz.at[zh], gz.at[zh], gz_send.at[i], gz_recv.at[zh], peer)
        cp.start()
        sent.append(cp)

    for i, f in enumerate(OCT_FAR):
        q, peer = oct_of(f)
        send(pp.at[q], r8.at[q], p8_send.at[i], p8_recv.at[q], peer).wait_recv()
    psum = r8[0]
    for q in range(1, 8):
        psum = psum + r8[q]
    zb[zh] = psum
    for i, j in enumerate(Z_FAR):
        w, peer = z_of(j)
        cp = send(zb.at[zh], zb.at[zh], z_send.at[i], z_recv.at[zh], peer)
        cp.start()
        sent.append(cp)

    for i, j in enumerate(Z_FAR):
        w, peer = z_of(j)
        send(zb.at[w], zb.at[w], z_send.at[i], z_recv.at[w], peer).wait_recv()
    psum = zb[0]
    for w in range(1, 8):
        psum = psum + zb[w]
    cb[m] = psum
    for i, f in enumerate(OCT_FAR):
        q, peer = oct_of(f)
        cp = send(cb.at[m], cb.at[m], c8_send.at[i], c8_recv.at[m], peer)
        cp.start()
        sent.append(cp)

    for i, j in enumerate(Z_FAR):
        w, peer = z_of(j)
        send(gz.at[w], gz.at[w], gz_send.at[i], gz_recv.at[w], peer).wait_recv()
    gsum = gz[0]
    for w in range(1, 8):
        gsum = gsum + gz[w]
    row_id = lax.broadcasted_iota(jnp.int32, (K, 128), 0)
    lane_id = lax.broadcasted_iota(jnp.int32, (K, 128), 1)
    full = jnp.concatenate(
        [gsum] + [pltpu.roll(gsum, 128 - K * b, 1) for b in range(1, 4)], axis=0
    )
    eye = jnp.where(lane_id == row_id + K, 1.0, 0.0)
    mat = jnp.where(lane_id < K, full, eye)
    for k in range(K - 1):
        row = mat[k : k + 1, :]
        col = mat[:, k : k + 1] / mat[k : k + 1, k : k + 1]
        mat = mat - jnp.where(row_id > k, col * row, 0.0)
    diag = jnp.sum(jnp.where(lane_id == row_id, mat, 0.0), axis=1, keepdims=True)
    mat = mat * lax.rsqrt(diag)
    inverse = pltpu.roll(mat, 128 - K, 1)[:, :K]

    for i, f in enumerate(OCT_FAR):
        q, peer = oct_of(f)
        send(cb.at[q], cb.at[q], c8_send.at[i], c8_recv.at[q], peer).wait_recv()
    for q in range(8):
        coef_out[:, 128 * q : 128 * q + 128] = jnp.dot(
            inverse, cb[q], preferred_element_type=jnp.float32, precision=lax.Precision.HIGHEST
        )
    for cp in sent:
        cp.wait_send()
    for cp in outs:
        cp.wait()


def per_device(snapshots, omega):
    rows = snapshots.shape[0] // 8
    cols = snapshots.shape[1]
    f32, bf16 = jnp.float32, jnp.bfloat16
    dma = pltpu.SemaphoreType.DMA
    return pl.pallas_call(
        kernel,
        name="pod",
        out_shape=(
            jax.ShapeDtypeStruct((K, snapshots.shape[0]), bf16),
            jax.ShapeDtypeStruct((K, cols), f32),
        ),
        in_specs=[pl.BlockSpec(memory_space=pl.ANY)] * 2,
        out_specs=(
            pl.BlockSpec(memory_space=pl.ANY),
            pl.BlockSpec(memory_space=pltpu.VMEM),
        ),
        scratch_shapes=[
            pltpu.VMEM((8, rows, cols), bf16),
            pltpu.VMEM((K, cols), jnp.int32),
            pltpu.VMEM((8, K, rows), f32),
            pltpu.VMEM((7, K, rows), f32),
            pltpu.VMEM((8, K, rows), bf16),
            pltpu.VMEM((8, K, 128), f32),
            pltpu.VMEM((8, K, 128), f32),
            pltpu.VMEM((8, K, 128), f32),
            pltpu.VMEM((8, K, 128), f32),
            pltpu.VMEM((8, 8, 128), f32),
            pltpu.VMEM((8, 8, 128), f32),
            dma((8,)), dma, dma((8,)),
        ]
        + [dma((7,)), dma((7,))]
        + [dma((7,)), dma((8,))] * 6,
        compiler_params=pltpu.CompilerParams(collective_id=0, has_side_effects=True),
    )(snapshots, omega)


def solution(mesh):
    return jax.shard_map(
        per_device,
        mesh=mesh,
        in_specs=(P("space", "tm"), P(None, "tm")),
        out_specs=(P(None, "space"), P(None, "tm")),
        check_vma=False,
    )
```

time: 724 us -> 50.9 us (0.07)
  waiting for transfers between devices: 483 us -> 0 us
  blocking collectives: 210 us -> 0 us
  Pallas kernels: 0 us -> 47 us
  between operations: 14.1 us -> 0.64 us
  matrix products: 10 us -> 0 us
  other arithmetic: 7.57 us -> 0 us
    psum x2 -> x0, waiting for transfers between devices: 483 us -> none  [the longest x1 383 us: per_device(): projection = lax.psum(proj_part, 'space')]
    psum x1 -> x0, blocking collectives: 210 us -> none  [per_device(): gram = lax.psum(gram_part, 'space')]
    pallas_call x0 -> x1, Pallas kernels: none -> 47 us  [per_device(): pl.pallas_call(kernel, name='pod', out_shape=(jax.ShapeDtypeStruct((K, sn...]
    dot_general x3 -> x0, matrix products: 8.15 us -> none  [the longest x1 4.31 us: per_device(): lax.dot_general(signs, snapshots, (((1,), (1,)), ((), ())), preferred_ele...]
  transfers between devices with their start and end apart: 2 -> 0, of which waited for: 2 -> 0; matrix products, arithmetic and copies ran while one was open for 0% -> 0% of each run, Pallas kernels for 0% -> 0%
where the time goes in v1:
time: 50.9 us; the launch traced here: 50.8 us
  Pallas kernels  47 us (92%)
  local copies, waits for them, and re-layouts  3.14 us (6%)
  between operations  0.64 us (1%)
    pallas_call x1, Pallas kernels, per_device(): pl.pallas_call(kernel, name='pod', out_shape=(jax.ShapeDtypeStruct((K, sn...  47 us
    unnamed x2, local copies, waits for them, and re-layouts  3.14 us

profile of v1, /device:TPU:1, one launch (start us, length us, event | category | flops | bytes accessed | tf_op | source)
XLA Modules:
  0.0 50.8 jit_solution(5595557689006893508)
XLA Ops:
  0.6 47.0 %pod.1 = (bf16[32,2048]{1,0:T(8,128)(2,1)}, f32[32,1024]{1,0:T(8,128)}) custom-call(bf16[2048,1024]{1,0:T(8,128)(2,1)} %snap.1, s32[32,1024]{1,0:T(8,128)} %omega.1), custom_call_target="tpu_custom_call" | custom-call | tf_op jit(solution)/shard_map/pod/pallas_call | solution.py:213
  47.6 1.6 %copy.6 = bf16[32,2048]{1,0:T(8,128)(2,1)} copy(bf16[32,2048]{1,0:T(8,128)(2,1)} %get-tuple-element.4) | data formatting | bytes 262144
  49.2 1.6 %copy.7 = f32[32,1024]{1,0:T(8,128)} copy(f32[32,1024]{1,0:T(8,128)} %get-tuple-element.5) | data formatting | bytes 262144

commit v2 on v1

--- a/solution.py
+++ b/solution.py
@@ -18,9 +18,9 @@
 
 
 def kernel(
-    snap, omega, sketch_out, coef_out,
-    a, om, part, rs, sk, pp, r8, zb, cb, g8, gz,
-    in_sem, om_sem, out_sem,
+    snap, omega, sk, coef,
+    a, om, part, rs, pp, r8, zb, cb, g8, gz,
+    in_sem, om_sem, near_sem, far_sem,
     rs_send, rs_recv, ag_send, ag_recv, p8_send, p8_recv, z_send, z_recv,
     c8_send, c8_recv, g8_send, g8_recv, gz_send, gz_recv,
 ):
@@ -55,9 +55,16 @@
 
     barrier = pltpu.get_barrier_semaphore()
     peers = [(s, tm_of(off)) for off in TM_FAR]
-    peers += [oct_of(f)[1] for f in OCT_FAR] + [z_of(j)[1] for j in Z_FAR]
+    peers += [oct_of(f)[1] for f in OCT_FAR] + [z_of(j)[1] for j in (1, 7)]
     for peer in peers:
         pl.semaphore_signal(barrier, inc=1, device_id=peer, device_id_type=MESH)
+
+    def tell(sem, steps):
+        for j in steps:
+            pl.semaphore_signal(sem, inc=1, device_id=z_of(j)[1], device_id_type=MESH)
+
+    def rows_of(d):
+        return sk.at[:, pl.ds(pl.multiple_of(d * rows, rows), rows)]
 
     def send(src, dst, send_sem, recv_sem, peer):
         return pltpu.make_async_remote_copy(
@@ -67,44 +74,42 @@
 
     om_copy.wait()
     signs = om[...].astype(jnp.float32).astype(jnp.bfloat16)
+    sent = []
+    rs_copies = []
     for i, d in enumerate(order):
         loads[i].wait()
         part[i] = lax.dot_general(
             signs, a[d], (((1,), (1,)), ((), ())), preferred_element_type=jnp.float32
         )
-    pl.semaphore_wait(barrier, len(peers))
-    sent = []
-    rs_copies = []
-    for i, off in enumerate(TM_FAR):
-        cp = send(part.at[i], rs.at[i], rs_send.at[i], rs_recv.at[i], (s, order[i]))
-        cp.start()
-        rs_copies.append(cp)
+        if i == 0:
+            pl.semaphore_wait(barrier, len(peers))
+            tell(near_sem, (1, 7))
+        if i < 7:
+            cp = send(part.at[i], rs.at[i], rs_send.at[i], rs_recv.at[i], (s, d))
+            cp.start()
+            rs_copies.append(cp)
     sent += rs_copies
+    pl.semaphore_wait(near_sem, 2)
+    tell(far_sem, (2, 6))
 
     total = part[7]
     for i in (5, 6, 4, 3, 1, 2, 0):
         rs_copies[i].wait_recv()
         total = total + rs[i]
     factor = SNAP ** (-0.5)
-    sk[t] = (total * factor).astype(jnp.bfloat16)
+    sk[:, pl.ds(pl.multiple_of(t * rows, rows), rows)] = (total * factor).astype(jnp.bfloat16)
     for i, off in enumerate(TM_FAR):
-        cp = send(sk.at[t], sk.at[t], ag_send.at[i], ag_recv.at[t], (s, order[i]))
+        cp = send(rows_of(t), rows_of(t), ag_send.at[i], ag_recv.at[t], (s, order[i]))
         cp.start()
         sent.append(cp)
 
     proj = None
     gram = None
-    outs = []
     for i in (7, 5, 6, 4, 3, 1, 2, 0):
         d = order[i]
         if i < 7:
-            send(sk.at[d], sk.at[d], ag_send.at[i], ag_recv.at[d], (s, d)).wait_recv()
-        cp = pltpu.make_async_copy(
-            sk.at[d], sketch_out.at[:, pl.ds(pl.multiple_of(d * rows, rows), rows)], out_sem.at[i]
-        )
-        cp.start()
-        outs.append(cp)
-        block = sk[d]
+            send(rows_of(d), rows_of(d), ag_send.at[i], ag_recv.at[d], (s, d)).wait_recv()
+        block = sk[:, pl.ds(pl.multiple_of(d * rows, rows), rows)]
         wide = jnp.concatenate([block] * 4, axis=0)
         g = lax.dot_general(
             block, wide, (((1,), (1,)), ((), ())), preferred_element_type=jnp.float32
@@ -139,6 +144,7 @@
     for q in range(1, 8):
         gsum = gsum + g8[q]
     gz[zh] = gsum
+    pl.semaphore_wait(far_sem, 2)
     for i, j in enumerate(Z_FAR):
         w, peer = z_of(j)
         cp = send(gz.at[zh], gz.at[zh], gz_send.at[i], gz_recv.at[zh], peer)
@@ -155,19 +161,6 @@
     for i, j in enumerate(Z_FAR):
         w, peer = z_of(j)
         cp = send(zb.at[zh], zb.at[zh], z_send.at[i], z_recv.at[zh], peer)
-        cp.start()
-        sent.append(cp)
-
-    for i, j in enumerate(Z_FAR):
-        w, peer = z_of(j)
-        send(zb.at[w], zb.at[w], z_send.at[i], z_recv.at[w], peer).wait_recv()
-    psum = zb[0]
-    for w in range(1, 8):
-        psum = psum + zb[w]
-    cb[m] = psum
-    for i, f in enumerate(OCT_FAR):
-        q, peer = oct_of(f)
-        cp = send(cb.at[m], cb.at[m], c8_send.at[i], c8_recv.at[m], peer)
         cp.start()
         sent.append(cp)
 
@@ -192,55 +185,67 @@
     mat = mat * lax.rsqrt(diag)
     inverse = pltpu.roll(mat, 128 - K, 1)[:, :K]
 
+    for i, j in enumerate(Z_FAR):
+        w, peer = z_of(j)
+        send(zb.at[w], zb.at[w], z_send.at[i], z_recv.at[w], peer).wait_recv()
+    psum = zb[0]
+    for w in range(1, 8):
+        psum = psum + zb[w]
+    cb[m] = jnp.dot(
+        inverse, psum, preferred_element_type=jnp.float32, precision=lax.Precision.HIGHEST
+    ).astype(jnp.bfloat16)
+    for i, f in enumerate(OCT_FAR):
+        q, peer = oct_of(f)
+        cp = send(cb.at[m], cb.at[m], c8_send.at[i], c8_recv.at[m], peer)
+        cp.start()
+        sent.append(cp)
+
     for i, f in enumerate(OCT_FAR):
         q, peer = oct_of(f)
         send(cb.at[q], cb.at[q], c8_send.at[i], c8_recv.at[q], peer).wait_recv()
     for q in range(8):
-        coef_out[:, 128 * q : 128 * q + 128] = jnp.dot(
-            inverse, cb[q], preferred_element_type=jnp.float32, precision=lax.Precision.HIGHEST
-        )
+        coef[:, 128 * q : 128 * q + 128] = cb[q].astype(jnp.float32)
     for cp in sent:
         cp.wait_send()
-    for cp in outs:
-        cp.wait()
 
 
 def per_device(snapshots, omega):
     rows = snapshots.shape[0] // 8
     cols = snapshots.shape[1]
     f32, bf16 = jnp.float32, jnp.bfloat16
-    dma = pltpu.SemaphoreType.DMA
+    dma, regular = pltpu.SemaphoreType.DMA, pltpu.SemaphoreType.REGULAR
+    whole = pl.BlockSpec(memory_space=pltpu.VMEM)
     return pl.pallas_call(
         kernel,
         name="pod",
         out_shape=(
-            jax.ShapeDtypeStruct((K, snapshots.shape[0]), bf16),
-            jax.ShapeDtypeStruct((K, cols), f32),
+            pltpu.VMEM((K, snapshots.shape[0]), bf16),
+            pltpu.VMEM((K, cols), f32),
         ),
-        in_specs=[pl.BlockSpec(memory_space=pl.ANY)] * 2,
-        out_specs=(
-            pl.BlockSpec(memory_space=pl.ANY),
-            pl.BlockSpec(memory_space=pltpu.VMEM),
-        ),
+        in_specs=[pl.BlockSpec(memory_space=pltpu.HBM)] * 2,
+        out_specs=(whole, whole),
         scratch_shapes=[
             pltpu.VMEM((8, rows, cols), bf16),
             pltpu.VMEM((K, cols), jnp.int32),
             pltpu.VMEM((8, K, rows), f32),
             pltpu.VMEM((7, K, rows), f32),
-            pltpu.VMEM((8, K, rows), bf16),
             pltpu.VMEM((8, K, 128), f32),
             pltpu.VMEM((8, K, 128), f32),
             pltpu.VMEM((8, K, 128), f32),
-            pltpu.VMEM((8, K, 128), f32),
+            pltpu.VMEM((8, K, 128), bf16),
             pltpu.VMEM((8, 8, 128), f32),
             pltpu.VMEM((8, 8, 128), f32),
-            dma((8,)), dma, dma((8,)),
+            dma((8,)), dma, regular, regular,
         ]
         + [dma((7,)), dma((7,))]
         + [dma((7,)), dma((8,))] * 6,
-        compiler_params=pltpu.CompilerParams(collective_id=0, has_side_effects=True),
-    )(snapshots, omega)
-
+        compiler_params=pltpu.CompilerParams(
+            collective_id=0, has_side_effects=True, vmem_limit_bytes=48 * 2**20
+        ),
+    )(
+        pltpu.with_memory_space_constraint(snapshots, pltpu.HBM),
+        pltpu.with_memory_space_constraint(omega, pltpu.HBM),
+    )
 
 def solution(mesh):
     return jax.shard_map(

time: 50.9 us -> 47.5 us (0.933)
  local copies, waits for them, and re-layouts: 3.14 us -> 1.31 us
  Pallas kernels: 47 us -> 45.5 us
    unnamed x2, local copies, waits for them, and re-layouts: 3.14 us -> 1.31 us
    pallas_call x1, Pallas kernels: 47 us -> 45.5 us  [per_device(): pl.pallas_call(kernel, name='pod', out_shape=(pltpu.VMEM((K, snapshots.sh...]
where the time goes in v2:
time: 47.5 us; the launch traced here: 47.4 us
  Pallas kernels  45.5 us (96%)
  local copies, waits for them, and re-layouts  1.31 us (3%)
  between operations  0.64 us (1%)
    pallas_call x1, Pallas kernels, per_device(): pl.pallas_call(kernel, name='pod', out_shape=(pltpu.VMEM((K, snapshots.sh...  45.5 us
    unnamed x2, local copies, waits for them, and re-layouts  1.31 us

profile of v2, /device:TPU:1, one launch (start us, length us, event | category | flops | bytes accessed | tf_op | source)
XLA Modules:
  0.0 47.4 jit_solution(3914403277206599623)
XLA Ops:
  0.6 45.5 %pod.1 = (bf16[32,2048]{1,0:T(8,128)(2,1)S(1)}, f32[32,1024]{1,0:T(8,128)S(1)}) custom-call(bf16[2048,1024]{1,0:T(8,128)(2,1)} %snap.1, s32[32,1024]{1,0:T(8,128)} %omega.1), custom_call_target="tpu_custom_call" | custom-call | tf_op jit(solution)/shard_map/pod/pallas_call | solution.py:218
  46.1 0.7 %copy.6 = bf16[32,2048]{1,0:T(8,128)(2,1)} copy(bf16[32,2048]{1,0:T(8,128)(2,1)S(1)} %get-tuple-element.2) | data formatting | bytes 262144
  46.8 0.7 %copy.7 = f32[32,1024]{1,0:T(8,128)} copy(f32[32,1024]{1,0:T(8,128)S(1)} %get-tuple-element.3) | data formatting | bytes 262144

commit v3 on v2

--- a/solution.py
+++ b/solution.py
@@ -17,12 +17,23 @@
     return (bit + f) % 2
 
 
+def to_int16(x):
+    top = jnp.max(jnp.max(jnp.abs(x), axis=0, keepdims=True), axis=1, keepdims=True)
+    top = jnp.where(top > 0.0, top, 1.0)
+    units = jnp.round(x * (32766.0 / top)).astype(jnp.int32).astype(jnp.int16)
+    return units, jnp.broadcast_to(top * (1.0 / 32766.0), (1, 128))
+
+
+def from_int16(units, step):
+    return units.astype(jnp.int32).astype(jnp.float32) * step
+
+
 def kernel(
     snap, omega, sk, coef,
-    a, om, part, rs, pp, r8, zb, cb, g8, gz,
+    a, om, part, rs, pp, r8, rst, zb, zs, cb, g8, gz,
     in_sem, om_sem, near_sem, far_sem,
     rs_send, rs_recv, ag_send, ag_recv, p8_send, p8_recv, z_send, z_recv,
-    c8_send, c8_recv, g8_send, g8_recv, gz_send, gz_recv,
+    c8_send, c8_recv, g8_send, g8_recv, gz_send, gz_recv, zs_send, zs_recv, rst_send, rst_recv,
 ):
     s, t = lax.axis_index("space"), lax.axis_index("tm")
     z, xl, c = s // 4, (s // 2) % 2, s % 2
@@ -44,21 +55,22 @@
 
     om_copy = pltpu.make_async_copy(omega, om, om_sem)
     om_copy.start()
-    order = [tm_of(off) for off in TM_FAR] + [t]
-    loads = []
-    for i, d in enumerate(order):
-        cp = pltpu.make_async_copy(
-            snap.at[pl.ds(pl.multiple_of(d * rows, rows), rows), :], a.at[d], in_sem.at[i]
-        )
-        cp.start()
-        loads.append(cp)
-
     barrier = pltpu.get_barrier_semaphore()
     peers = [(s, tm_of(off)) for off in TM_FAR]
     peers += [oct_of(f)[1] for f in OCT_FAR] + [z_of(j)[1] for j in (1, 7)]
     for peer in peers:
         pl.semaphore_signal(barrier, inc=1, device_id=peer, device_id_type=MESH)
 
+    order = [tm_of(off) for off in TM_FAR] + [t]
+    loads = [
+        pltpu.make_async_copy(
+            snap.at[pl.ds(pl.multiple_of(d * rows, rows), rows), :], a.at[d], in_sem.at[i]
+        )
+        for i, d in enumerate(order)
+    ]
+    for cp in loads[:4]:
+        cp.start()
+
     def tell(sem, steps):
         for j in steps:
             pl.semaphore_signal(sem, inc=1, device_id=z_of(j)[1], device_id_type=MESH)
@@ -73,19 +85,23 @@
         )
 
     om_copy.wait()
+    for cp in loads[4:]:
+        cp.start()
     signs = om[...].astype(jnp.float32).astype(jnp.bfloat16)
     sent = []
     rs_copies = []
-    for i, d in enumerate(order):
-        loads[i].wait()
-        part[i] = lax.dot_general(
-            signs, a[d], (((1,), (1,)), ((), ())), preferred_element_type=jnp.float32
-        )
-        if i == 0:
+    for first in (0, 4):
+        for i in range(first, first + 4):
+            loads[i].wait()
+        for i in range(first, first + 4):
+            part[i] = lax.dot_general(
+                signs, a[order[i]], (((1,), (1,)), ((), ())), preferred_element_type=jnp.float32
+            )
+        if first == 0:
             pl.semaphore_wait(barrier, len(peers))
             tell(near_sem, (1, 7))
-        if i < 7:
-            cp = send(part.at[i], rs.at[i], rs_send.at[i], rs_recv.at[i], (s, d))
+        for i in range(first, min(first + 4, 7)):
+            cp = send(part.at[i], rs.at[i], rs_send.at[i], rs_recv.at[i], (s, order[i]))
             cp.start()
             rs_copies.append(cp)
     sent += rs_copies
@@ -128,12 +144,16 @@
         cp = send(g8.at[m], g8.at[m], g8_send.at[i], g8_recv.at[m], peer)
         cp.start()
         sent.append(cp)
+    units, rst[m] = to_int16(proj)
     for q in range(8):
-        pp[q] = proj[:, 128 * q : 128 * q + 128]
+        pp[q] = units[:, 128 * q : 128 * q + 128]
     r8[m] = pp[m]
     for i, f in enumerate(OCT_FAR):
         q, peer = oct_of(f)
         cp = send(pp.at[q], r8.at[m], p8_send.at[i], p8_recv.at[m], peer)
+        cp.start()
+        sent.append(cp)
+        cp = send(rst.at[m], rst.at[m], rst_send.at[i], rst_recv.at[m], peer)
         cp.start()
         sent.append(cp)
 
@@ -154,13 +174,17 @@
     for i, f in enumerate(OCT_FAR):
         q, peer = oct_of(f)
         send(pp.at[q], r8.at[q], p8_send.at[i], p8_recv.at[q], peer).wait_recv()
-    psum = r8[0]
+        send(rst.at[q], rst.at[q], rst_send.at[i], rst_recv.at[q], peer).wait_recv()
+    psum = from_int16(r8[0], rst[0])
     for q in range(1, 8):
-        psum = psum + r8[q]
-    zb[zh] = psum
+        psum = psum + from_int16(r8[q], rst[q])
+    zb[zh], zs[zh] = to_int16(psum)
     for i, j in enumerate(Z_FAR):
         w, peer = z_of(j)
         cp = send(zb.at[zh], zb.at[zh], z_send.at[i], z_recv.at[zh], peer)
+        cp.start()
+        sent.append(cp)
+        cp = send(zs.at[zh], zs.at[zh], zs_send.at[i], zs_recv.at[zh], peer)
         cp.start()
         sent.append(cp)
 
@@ -177,10 +201,16 @@
     )
     eye = jnp.where(lane_id == row_id + K, 1.0, 0.0)
     mat = jnp.where(lane_id < K, full, eye)
-    for k in range(K - 1):
-        row = mat[k : k + 1, :]
-        col = mat[:, k : k + 1] / mat[k : k + 1, k : k + 1]
-        mat = mat - jnp.where(row_id > k, col * row, 0.0)
+    for panel in range(0, K, 8):
+        cols = [
+            jnp.broadcast_to(mat[:, k : k + 1], (K, 128)) for k in range(panel, panel + 8)
+        ]
+        for j in range(8):
+            k = panel + j
+            ratio = jnp.where(row_id > k, cols[j] * (1.0 / cols[j][k : k + 1, :]), 0.0)
+            for l in range(j + 1, 8):
+                cols[l] = cols[l] - ratio * cols[l][k : k + 1, :]
+            mat = mat - ratio * mat[k : k + 1, :]
     diag = jnp.sum(jnp.where(lane_id == row_id, mat, 0.0), axis=1, keepdims=True)
     mat = mat * lax.rsqrt(diag)
     inverse = pltpu.roll(mat, 128 - K, 1)[:, :K]
@@ -188,9 +218,10 @@
     for i, j in enumerate(Z_FAR):
         w, peer = z_of(j)
         send(zb.at[w], zb.at[w], z_send.at[i], z_recv.at[w], peer).wait_recv()
-    psum = zb[0]
+        send(zs.at[w], zs.at[w], zs_send.at[i], zs_recv.at[w], peer).wait_recv()
+    psum = from_int16(zb[0], zs[0])
     for w in range(1, 8):
-        psum = psum + zb[w]
+        psum = psum + from_int16(zb[w], zs[w])
     cb[m] = jnp.dot(
         inverse, psum, preferred_element_type=jnp.float32, precision=lax.Precision.HIGHEST
     ).astype(jnp.bfloat16)
@@ -207,6 +238,17 @@
         coef[:, 128 * q : 128 * q + 128] = cb[q].astype(jnp.float32)
     for cp in sent:
         cp.wait_send()
+
+
+def store(sk, coef, sketch_out, coef_out, sem):
+    copies = [
+        pltpu.make_async_copy(sk, sketch_out, sem.at[0]),
+        pltpu.make_async_copy(coef, coef_out, sem.at[1]),
+    ]
+    for cp in copies:
+        cp.start()
+    for cp in copies:
+        cp.wait()
 
 
 def per_device(snapshots, omega):
@@ -215,7 +257,7 @@
     f32, bf16 = jnp.float32, jnp.bfloat16
     dma, regular = pltpu.SemaphoreType.DMA, pltpu.SemaphoreType.REGULAR
     whole = pl.BlockSpec(memory_space=pltpu.VMEM)
-    return pl.pallas_call(
+    sk, coef = pl.pallas_call(
         kernel,
         name="pod",
         out_shape=(
@@ -229,16 +271,18 @@
             pltpu.VMEM((K, cols), jnp.int32),
             pltpu.VMEM((8, K, rows), f32),
             pltpu.VMEM((7, K, rows), f32),
-            pltpu.VMEM((8, K, 128), f32),
-            pltpu.VMEM((8, K, 128), f32),
-            pltpu.VMEM((8, K, 128), f32),
+            pltpu.VMEM((8, K, 128), jnp.int16),
+            pltpu.VMEM((8, K, 128), jnp.int16),
+            pltpu.VMEM((8, 1, 128), f32),
+            pltpu.VMEM((8, K, 128), jnp.int16),
+            pltpu.VMEM((8, 1, 128), f32),
             pltpu.VMEM((8, K, 128), bf16),
             pltpu.VMEM((8, 8, 128), f32),
             pltpu.VMEM((8, 8, 128), f32),
             dma((8,)), dma, regular, regular,
         ]
         + [dma((7,)), dma((7,))]
-        + [dma((7,)), dma((8,))] * 6,
+        + [dma((7,)), dma((8,))] * 8,
         compiler_params=pltpu.CompilerParams(
             collective_id=0, has_side_effects=True, vmem_limit_bytes=48 * 2**20
         ),
@@ -246,6 +290,18 @@
         pltpu.with_memory_space_constraint(snapshots, pltpu.HBM),
         pltpu.with_memory_space_constraint(omega, pltpu.HBM),
     )
+    return pl.pallas_call(
+        store,
+        name="store",
+        out_shape=(
+            jax.ShapeDtypeStruct(sk.shape, sk.dtype),
+            jax.ShapeDtypeStruct(coef.shape, coef.dtype),
+        ),
+        in_specs=[whole] * 2,
+        out_specs=(pl.BlockSpec(memory_space=pl.ANY),) * 2,
+        scratch_shapes=[dma((2,))],
+        compiler_params=pltpu.CompilerParams(vmem_limit_bytes=4 * 2**20),
+    )(sk, coef)
 
 def solution(mesh):
     return jax.shard_map(

time: 47.5 us -> 45.3 us (0.954)
  local copies, waits for them, and re-layouts: 1.31 us -> 0 us
  Pallas kernels: 45.5 us -> 44.5 us
    pallas_call x1, Pallas kernels: 45.5 us -> 43.8 us  [per_device(): pl.pallas_call(kernel, name='pod', out_shape=(pltpu.VMEM((K, snapshots.sh...]
    unnamed x2 -> x0, local copies, waits for them, and re-layouts: 1.31 us -> none
    pallas_call x0 -> x1, Pallas kernels: none -> 0.72 us  [per_device(): pl.pallas_call(store, name='store', out_shape=(jax.ShapeDtypeStruct(sk.sh...]
where the time goes in v3:
time: 45.3 us; the launch traced here: 45.2 us
  Pallas kernels  44.5 us (98%)
  between operations  0.64 us (1%)
    pallas_call x1, Pallas kernels, per_device(): pl.pallas_call(kernel, name='pod', out_shape=(pltpu.VMEM((K, snapshots.sh...  43.8 us

profile of v3, /device:TPU:1, one launch (start us, length us, event | category | flops | bytes accessed | tf_op | source)
XLA Modules:
  0.0 45.2 jit_solution(4359696947704069991)
XLA Ops:
  0.6 43.8 %pod.1 = (bf16[32,2048]{1,0:T(8,128)(2,1)S(1)}, f32[32,1024]{1,0:T(8,128)S(1)}) custom-call(bf16[2048,1024]{1,0:T(8,128)(2,1)} %snap.1, s32[32,1024]{1,0:T(8,128)} %omega.1), custom_call_target="tpu_custom_call" | custom-call | tf_op jit(solution)/shard_map/pod/pallas_call | solution.py:260
  44.4 0.7 %store.1 = (bf16[32,2048]{1,0:T(8,128)(2,1)}, f32[32,1024]{1,0:T(8,128)}) custom-call(bf16[32,2048]{1,0:T(8,128)(2,1)S(1)} %get-tuple-element.4.sk, f32[32,1024]{1,0:T(8,128)S(1)} %get-tuple-element.5.coef), custom_call_target="tpu_custom_call" | custom-call | tf_op jit(solution)/shard_map/store/pallas_call | solution.py:293

commit v4 on v3

--- a/solution.py
+++ b/solution.py
@@ -64,7 +64,7 @@
     order = [tm_of(off) for off in TM_FAR] + [t]
     loads = [
         pltpu.make_async_copy(
-            snap.at[pl.ds(pl.multiple_of(d * rows, rows), rows), :], a.at[d], in_sem.at[i]
+            snap.at[pl.ds(pl.multiple_of(d * rows, rows), rows), :], a.at[d], in_sem.at[i // 4]
         )
         for i, d in enumerate(order)
     ]
@@ -84,15 +84,19 @@
             device_id=peer, device_id_type=MESH,
         )
 
+    def arrived(blocks, send_sem, recv_sem):
+        send(blocks, blocks, send_sem, recv_sem, peers[0]).wait_recv()
+
+    def left(blocks, send_sem, recv_sem):
+        send(blocks, blocks, send_sem, recv_sem, peers[0]).wait_send()
+
     om_copy.wait()
     for cp in loads[4:]:
         cp.start()
     signs = om[...].astype(jnp.float32).astype(jnp.bfloat16)
-    sent = []
-    rs_copies = []
     for first in (0, 4):
-        for i in range(first, first + 4):
-            loads[i].wait()
+        four = a.at[pl.ds(0, 4)]
+        pltpu.make_async_copy(four, four, in_sem.at[first // 4]).wait()
         for i in range(first, first + 4):
             part[i] = lax.dot_general(
                 signs, a[order[i]], (((1,), (1,)), ((), ())), preferred_element_type=jnp.float32
@@ -101,30 +105,27 @@
             pl.semaphore_wait(barrier, len(peers))
             tell(near_sem, (1, 7))
         for i in range(first, min(first + 4, 7)):
-            cp = send(part.at[i], rs.at[i], rs_send.at[i], rs_recv.at[i], (s, order[i]))
+            cp = send(part.at[i], rs.at[i], rs_send, rs_recv, (s, order[i]))
             cp.start()
-            rs_copies.append(cp)
-    sent += rs_copies
     pl.semaphore_wait(near_sem, 2)
     tell(far_sem, (2, 6))
 
     total = part[7]
-    for i in (5, 6, 4, 3, 1, 2, 0):
-        rs_copies[i].wait_recv()
+    arrived(rs, rs_send, rs_recv)
+    for i in range(7):
         total = total + rs[i]
     factor = SNAP ** (-0.5)
     sk[:, pl.ds(pl.multiple_of(t * rows, rows), rows)] = (total * factor).astype(jnp.bfloat16)
     for i, off in enumerate(TM_FAR):
-        cp = send(rows_of(t), rows_of(t), ag_send.at[i], ag_recv.at[t], (s, order[i]))
-        cp.start()
-        sent.append(cp)
+        cp = send(rows_of(t), rows_of(t), ag_send, ag_recv.at[t], (s, order[i]))
+        cp.start()
 
     proj = None
     gram = None
     for i in (7, 5, 6, 4, 3, 1, 2, 0):
         d = order[i]
         if i < 7:
-            send(rows_of(d), rows_of(d), ag_send.at[i], ag_recv.at[d], (s, d)).wait_recv()
+            send(rows_of(d), rows_of(d), ag_send, ag_recv.at[d], (s, d)).wait_recv()
         block = sk[:, pl.ds(pl.multiple_of(d * rows, rows), rows)]
         wide = jnp.concatenate([block] * 4, axis=0)
         g = lax.dot_general(
@@ -141,25 +142,20 @@
     g8[m] = packed
     for i, f in enumerate(OCT_FAR):
         q, peer = oct_of(f)
-        cp = send(g8.at[m], g8.at[m], g8_send.at[i], g8_recv.at[m], peer)
-        cp.start()
-        sent.append(cp)
+        cp = send(g8.at[m], g8.at[m], g8_send, g8_recv, peer)
+        cp.start()
     units, rst[m] = to_int16(proj)
     for q in range(8):
         pp[q] = units[:, 128 * q : 128 * q + 128]
     r8[m] = pp[m]
     for i, f in enumerate(OCT_FAR):
         q, peer = oct_of(f)
-        cp = send(pp.at[q], r8.at[m], p8_send.at[i], p8_recv.at[m], peer)
-        cp.start()
-        sent.append(cp)
-        cp = send(rst.at[m], rst.at[m], rst_send.at[i], rst_recv.at[m], peer)
-        cp.start()
-        sent.append(cp)
-
-    for i, f in enumerate(OCT_FAR):
-        q, peer = oct_of(f)
-        send(g8.at[q], g8.at[q], g8_send.at[i], g8_recv.at[q], peer).wait_recv()
+        cp = send(pp.at[q], r8.at[m], p8_send, p8_recv, peer)
+        cp.start()
+        cp = send(rst.at[m], rst.at[m], rst_send, rst_recv, peer)
+        cp.start()
+
+    arrived(g8.at[pl.ds(0, 7)], g8_send, g8_recv)
     gsum = g8[0]
     for q in range(1, 8):
         gsum = gsum + g8[q]
@@ -167,30 +163,23 @@
     pl.semaphore_wait(far_sem, 2)
     for i, j in enumerate(Z_FAR):
         w, peer = z_of(j)
-        cp = send(gz.at[zh], gz.at[zh], gz_send.at[i], gz_recv.at[zh], peer)
-        cp.start()
-        sent.append(cp)
-
-    for i, f in enumerate(OCT_FAR):
-        q, peer = oct_of(f)
-        send(pp.at[q], r8.at[q], p8_send.at[i], p8_recv.at[q], peer).wait_recv()
-        send(rst.at[q], rst.at[q], rst_send.at[i], rst_recv.at[q], peer).wait_recv()
+        cp = send(gz.at[zh], gz.at[zh], gz_send, gz_recv, peer)
+        cp.start()
+
+    arrived(r8.at[pl.ds(0, 7)], p8_send, p8_recv)
+    arrived(rst.at[pl.ds(0, 7)], rst_send, rst_recv)
     psum = from_int16(r8[0], rst[0])
     for q in range(1, 8):
         psum = psum + from_int16(r8[q], rst[q])
     zb[zh], zs[zh] = to_int16(psum)
     for i, j in enumerate(Z_FAR):
         w, peer = z_of(j)
-        cp = send(zb.at[zh], zb.at[zh], z_send.at[i], z_recv.at[zh], peer)
-        cp.start()
-        sent.append(cp)
-        cp = send(zs.at[zh], zs.at[zh], zs_send.at[i], zs_recv.at[zh], peer)
-        cp.start()
-        sent.append(cp)
-
-    for i, j in enumerate(Z_FAR):
-        w, peer = z_of(j)
-        send(gz.at[w], gz.at[w], gz_send.at[i], gz_recv.at[w], peer).wait_recv()
+        cp = send(zb.at[zh], zb.at[zh], z_send, z_recv, peer)
+        cp.start()
+        cp = send(zs.at[zh], zs.at[zh], zs_send, zs_recv, peer)
+        cp.start()
+
+    arrived(gz.at[pl.ds(0, 7)], gz_send, gz_recv)
     gsum = gz[0]
     for w in range(1, 8):
         gsum = gsum + gz[w]
@@ -215,10 +204,8 @@
     mat = mat * lax.rsqrt(diag)
     inverse = pltpu.roll(mat, 128 - K, 1)[:, :K]
 
-    for i, j in enumerate(Z_FAR):
-        w, peer = z_of(j)
-        send(zb.at[w], zb.at[w], z_send.at[i], z_recv.at[w], peer).wait_recv()
-        send(zs.at[w], zs.at[w], zs_send.at[i], zs_recv.at[w], peer).wait_recv()
+    arrived(zb.at[pl.ds(0, 7)], z_send, z_recv)
+    arrived(zs.at[pl.ds(0, 7)], zs_send, zs_recv)
     psum = from_int16(zb[0], zs[0])
     for w in range(1, 8):
         psum = psum + from_int16(zb[w], zs[w])
@@ -227,17 +214,19 @@
     ).astype(jnp.bfloat16)
     for i, f in enumerate(OCT_FAR):
         q, peer = oct_of(f)
-        cp = send(cb.at[m], cb.at[m], c8_send.at[i], c8_recv.at[m], peer)
-        cp.start()
-        sent.append(cp)
-
-    for i, f in enumerate(OCT_FAR):
-        q, peer = oct_of(f)
-        send(cb.at[q], cb.at[q], c8_send.at[i], c8_recv.at[q], peer).wait_recv()
+        cp = send(cb.at[m], cb.at[m], c8_send, c8_recv, peer)
+        cp.start()
+
+    arrived(cb.at[pl.ds(0, 7)], c8_send, c8_recv)
     for q in range(8):
         coef[:, 128 * q : 128 * q + 128] = cb[q].astype(jnp.float32)
-    for cp in sent:
-        cp.wait_send()
+    left(rs, rs_send, rs_recv)
+    left(sk.at[:, pl.ds(0, 7 * rows)], ag_send, ag_recv.at[0])
+    for blocks, send_sem, recv_sem in (
+        (g8, g8_send, g8_recv), (pp, p8_send, p8_recv), (rst, rst_send, rst_recv),
+        (gz, gz_send, gz_recv), (zb, z_send, z_recv), (zs, zs_send, zs_recv), (cb, c8_send, c8_recv),
+    ):
+        left(blocks.at[pl.ds(0, 7)], send_sem, recv_sem)
 
 
 def store(sk, coef, sketch_out, coef_out, sem):
@@ -279,10 +268,10 @@
             pltpu.VMEM((8, K, 128), bf16),
             pltpu.VMEM((8, 8, 128), f32),
             pltpu.VMEM((8, 8, 128), f32),
-            dma((8,)), dma, regular, regular,
+            dma((2,)), dma, regular, regular,
         ]
-        + [dma((7,)), dma((7,))]
-        + [dma((7,)), dma((8,))] * 8,
+        + [dma, dma, dma, dma((8,))]
+        + [dma] * 14,
         compiler_params=pltpu.CompilerParams(
             collective_id=0, has_side_effects=True, vmem_limit_bytes=48 * 2**20
         ),

time: 45.3 us -> 44.2 us (0.976)
  Pallas kernels: 44.5 us -> 43.4 us
    pallas_call x1, Pallas kernels: 43.8 us -> 42.7 us  [per_device(): pl.pallas_call(kernel, name='pod', out_shape=(pltpu.VMEM((K, snapshots.sh...]
where the time goes in v4:
time: 44.2 us; the launch traced here: 44 us
  Pallas kernels  43.4 us (98%)
  between operations  0.64 us (1%)
    pallas_call x1, Pallas kernels, per_device(): pl.pallas_call(kernel, name='pod', out_shape=(pltpu.VMEM((K, snapshots.sh...  42.7 us

profile of v4, /device:TPU:1, one launch (start us, length us, event | category | flops | bytes accessed | tf_op | source)
XLA Modules:
  0.0 44.0 jit_solution(6900525384931062146)
XLA Ops:
  0.6 42.7 %pod.1 = (bf16[32,2048]{1,0:T(8,128)(2,1)S(1)}, f32[32,1024]{1,0:T(8,128)S(1)}) custom-call(bf16[2048,1024]{1,0:T(8,128)(2,1)} %snap.1, s32[32,1024]{1,0:T(8,128)} %omega.1), custom_call_target="tpu_custom_call" | custom-call | tf_op jit(solution)/shard_map/pod/pallas_call | solution.py:249
  43.3 0.7 %store.1 = (bf16[32,2048]{1,0:T(8,128)(2,1)}, f32[32,1024]{1,0:T(8,128)}) custom-call(bf16[32,2048]{1,0:T(8,128)(2,1)S(1)} %get-tuple-element.4.sk, f32[32,1024]{1,0:T(8,128)S(1)} %get-tuple-element.5.coef), custom_call_target="tpu_custom_call" | custom-call | tf_op jit(solution)/shard_map/store/pallas_call | solution.py:282

commit v5 on v4

--- a/solution.py
+++ b/solution.py
@@ -30,10 +30,10 @@
 
 def kernel(
     snap, omega, sk, coef,
-    a, om, part, rs, pp, r8, rst, zb, zs, cb, g8, gz,
+    a, om, part, rs, pp, r8, rst, zb, zs, cb, g8, gz, gt,
     in_sem, om_sem, near_sem, far_sem,
     rs_send, rs_recv, ag_send, ag_recv, p8_send, p8_recv, z_send, z_recv,
-    c8_send, c8_recv, g8_send, g8_recv, gz_send, gz_recv, zs_send, zs_recv, rst_send, rst_recv,
+    c8_send, c8_recv, g8_send, g8_recv, gz_send, gz_recv, zs_send, zs_recv, rst_send, rst_recv, gt_send, gt_recv,
 ):
     s, t = lax.axis_index("space"), lax.axis_index("tm")
     z, xl, c = s // 4, (s // 2) % 2, s % 2
@@ -116,8 +116,9 @@
         total = total + rs[i]
     factor = SNAP ** (-0.5)
     sk[:, pl.ds(pl.multiple_of(t * rows, rows), rows)] = (total * factor).astype(jnp.bfloat16)
-    for i, off in enumerate(TM_FAR):
-        cp = send(rows_of(t), rows_of(t), ag_send, ag_recv.at[t], (s, order[i]))
+    for i in range(7):
+        peer = order[i] + c * (order[(i + 4) % 7] - order[i])
+        cp = send(rows_of(t), rows_of(t), ag_send, ag_recv.at[t], (s, peer))
         cp.start()
 
     proj = None
@@ -161,10 +162,11 @@
         gsum = gsum + g8[q]
     gz[zh] = gsum
     pl.semaphore_wait(far_sem, 2)
-    for i, j in enumerate(Z_FAR):
-        w, peer = z_of(j)
-        cp = send(gz.at[zh], gz.at[zh], gz_send, gz_recv, peer)
-        cp.start()
+
+    @pl.when(c == 1)
+    def _():
+        for j in Z_FAR:
+            send(gz.at[zh], gz.at[zh], gz_send, gz_recv, z_of(j)[1]).start()
 
     arrived(r8.at[pl.ds(0, 7)], p8_send, p8_recv)
     arrived(rst.at[pl.ds(0, 7)], rst_send, rst_recv)
@@ -179,10 +181,22 @@
         cp = send(zs.at[zh], zs.at[zh], zs_send, zs_recv, peer)
         cp.start()
 
-    arrived(gz.at[pl.ds(0, 7)], gz_send, gz_recv)
-    gsum = gz[0]
-    for w in range(1, 8):
-        gsum = gsum + gz[w]
+    other = (s + 1 - 2 * c, t)
+
+    @pl.when(c == 1)
+    def _():
+        arrived(gz.at[pl.ds(0, 7)], gz_send, gz_recv)
+        gsum = gz[0]
+        for w in range(1, 8):
+            gsum = gsum + gz[w]
+        gt[...] = gsum
+        send(gt, gt, gt_send, gt_recv, other).start()
+
+    @pl.when(c == 0)
+    def _():
+        arrived(gt, gt_send, gt_recv)
+
+    gsum = gt[...]
     row_id = lax.broadcasted_iota(jnp.int32, (K, 128), 0)
     lane_id = lax.broadcasted_iota(jnp.int32, (K, 128), 1)
     full = jnp.concatenate(
@@ -224,9 +238,14 @@
     left(sk.at[:, pl.ds(0, 7 * rows)], ag_send, ag_recv.at[0])
     for blocks, send_sem, recv_sem in (
         (g8, g8_send, g8_recv), (pp, p8_send, p8_recv), (rst, rst_send, rst_recv),
-        (gz, gz_send, gz_recv), (zb, z_send, z_recv), (zs, zs_send, zs_recv), (cb, c8_send, c8_recv),
+        (zb, z_send, z_recv), (zs, zs_send, zs_recv), (cb, c8_send, c8_recv),
     ):
         left(blocks.at[pl.ds(0, 7)], send_sem, recv_sem)
+
+    @pl.when(c == 1)
+    def _():
+        left(gz.at[pl.ds(0, 7)], gz_send, gz_recv)
+        left(gt, gt_send, gt_recv)
 
 
 def store(sk, coef, sketch_out, coef_out, sem):
@@ -268,10 +287,11 @@
             pltpu.VMEM((8, K, 128), bf16),
             pltpu.VMEM((8, 8, 128), f32),
             pltpu.VMEM((8, 8, 128), f32),
+            pltpu.VMEM((8, 128), f32),
             dma((2,)), dma, regular, regular,
         ]
         + [dma, dma, dma, dma((8,))]
-        + [dma] * 14,
+        + [dma] * 16,
         compiler_params=pltpu.CompilerParams(
             collective_id=0, has_side_effects=True, vmem_limit_bytes=48 * 2**20
         ),

time: 44.2 us -> 43.2 us (0.977)
  Pallas kernels: 43.4 us -> 42.4 us
    pallas_call x1, Pallas kernels: 42.7 us -> 41.7 us  [per_device(): pl.pallas_call(kernel, name='pod', out_shape=(pltpu.VMEM((K, snapshots.sh...]
where the time goes in v5:
time: 43.2 us; the launch traced here: 43 us
  Pallas kernels  42.4 us (98%)
  between operations  0.64 us (1%)
    pallas_call x1, Pallas kernels, per_device(): pl.pallas_call(kernel, name='pod', out_shape=(pltpu.VMEM((K, snapshots.sh...  41.7 us

profile of v5, /device:TPU:1, one launch (start us, length us, event | category | flops | bytes accessed | tf_op | source)
XLA Modules:
  0.0 43.0 jit_solution(15286823163553044258)
XLA Ops:
  0.6 41.7 %pod.1 = (bf16[32,2048]{1,0:T(8,128)(2,1)S(1)}, f32[32,1024]{1,0:T(8,128)S(1)}) custom-call(bf16[2048,1024]{1,0:T(8,128)(2,1)} %snap.1, s32[32,1024]{1,0:T(8,128)} %omega.1), custom_call_target="tpu_custom_call" | custom-call | tf_op jit(solution)/shard_map/pod/pallas_call | solution.py:268
  42.3 0.7 %store.1 = (bf16[32,2048]{1,0:T(8,128)(2,1)}, f32[32,1024]{1,0:T(8,128)}) custom-call(bf16[32,2048]{1,0:T(8,128)(2,1)S(1)} %get-tuple-element.4.sk, f32[32,1024]{1,0:T(8,128)S(1)} %get-tuple-element.5.coef), custom_call_target="tpu_custom_call" | custom-call | tf_op jit(solution)/shard_map/store/pallas_call | solution.py:302

commit v6 on v5

--- a/solution.py
+++ b/solution.py
@@ -174,8 +174,8 @@
     for q in range(1, 8):
         psum = psum + from_int16(r8[q], rst[q])
     zb[zh], zs[zh] = to_int16(psum)
-    for i, j in enumerate(Z_FAR):
-        w, peer = z_of(j)
+    for far, near in zip(Z_FAR, Z_FAR[::-1]):
+        w, peer = z_of(far + c * (near - far))
         cp = send(zb.at[zh], zb.at[zh], z_send, z_recv, peer)
         cp.start()
         cp = send(zs.at[zh], zs.at[zh], zs_send, zs_recv, peer)

time: 43.2 us -> 42.9 us (level)
  no operation moved by 1% of the time
where the time goes in v6:
time: 42.9 us; the launch traced here: 42.7 us
  Pallas kernels  42.1 us (98%)
  between operations  0.64 us (1%)
    pallas_call x1, Pallas kernels, per_device(): pl.pallas_call(kernel, name='pod', out_shape=(pltpu.VMEM((K, snapshots.sh...  41.4 us

profile of v6, /device:TPU:1, one launch (start us, length us, event | category | flops | bytes accessed | tf_op | source)
XLA Modules:
  0.0 42.7 jit_solution(8454758406277160023)
XLA Ops:
  0.6 41.4 %pod.1 = (bf16[32,2048]{1,0:T(8,128)(2,1)S(1)}, f32[32,1024]{1,0:T(8,128)S(1)}) custom-call(bf16[2048,1024]{1,0:T(8,128)(2,1)} %snap.1, s32[32,1024]{1,0:T(8,128)} %omega.1), custom_call_target="tpu_custom_call" | custom-call | tf_op jit(solution)/shard_map/pod/pallas_call | solution.py:268
  42.0 0.7 %store.1 = (bf16[32,2048]{1,0:T(8,128)(2,1)}, f32[32,1024]{1,0:T(8,128)}) custom-call(bf16[32,2048]{1,0:T(8,128)(2,1)S(1)} %get-tuple-element.4.sk, f32[32,1024]{1,0:T(8,128)S(1)} %get-tuple-element.5.coef), custom_call_target="tpu_custom_call" | custom-call | tf_op jit(solution)/shard_map/store/pallas_call | solution.py:302

commit v7 on v6

--- a/solution.py
+++ b/solution.py
@@ -227,7 +227,8 @@
         inverse, psum, preferred_element_type=jnp.float32, precision=lax.Precision.HIGHEST
     ).astype(jnp.bfloat16)
     for i, f in enumerate(OCT_FAR):
-        q, peer = oct_of(f)
+        (_, (sq, _)), (_, (su, _)) = oct_of(f), oct_of(OCT_FAR[6 - i])
+        peer = (su + c * (sq - su), t)
         cp = send(cb.at[m], cb.at[m], c8_send, c8_recv, peer)
         cp.start()
 

time: 42.9 us -> 42.9 us (level)
  no operation moved by 1% of the time
where the time goes in v7:
time: 42.9 us; the launch traced here: 42.8 us
  Pallas kernels  42.2 us (98%)
  between operations  0.64 us (1%)
    pallas_call x1, Pallas kernels, per_device(): pl.pallas_call(kernel, name='pod', out_shape=(pltpu.VMEM((K, snapshots.sh...  41.5 us

profile of v7, /device:TPU:1, one launch (start us, length us, event | category | flops | bytes accessed | tf_op | source)
XLA Modules:
  0.0 42.8 jit_solution(14636794144081325421)
XLA Ops:
  0.6 41.5 %pod.1 = (bf16[32,2048]{1,0:T(8,128)(2,1)S(1)}, f32[32,1024]{1,0:T(8,128)S(1)}) custom-call(bf16[2048,1024]{1,0:T(8,128)(2,1)} %snap.1, s32[32,1024]{1,0:T(8,128)} %omega.1), custom_call_target="tpu_custom_call" | custom-call | tf_op jit(solution)/shard_map/pod/pallas_call | solution.py:269
  42.1 0.7 %store.1 = (bf16[32,2048]{1,0:T(8,128)(2,1)}, f32[32,1024]{1,0:T(8,128)}) custom-call(bf16[32,2048]{1,0:T(8,128)(2,1)S(1)} %get-tuple-element.4.sk, f32[32,1024]{1,0:T(8,128)S(1)} %get-tuple-element.5.coef), custom_call_target="tpu_custom_call" | custom-call | tf_op jit(solution)/shard_map/store/pallas_call | solution.py:303
